TPU v7x, 32 devices: a whole 2x2x4 slice. The times are simulated.
32 devices in a mesh: blk: 4 (over x, core), ulysses: 8 (over z, y).
Axes of the slice: x: 2, y: 2, z: 4, core: 2. Of those that a mesh axis runs over, the one named last changes fastest.
Arguments:
- query_rows: bfloat16 [32, 4096, 128], P(None, ('blk', 'ulysses')), may hold values from -160 to 160
- out_grad: bfloat16 [32, 4096, 128], P(None, ('blk', 'ulysses')), may hold values from -6 to 6
- key_rows: bfloat16 [32, 512, 128], P(None, 'blk'), may hold values from -6 to 6
- value_rows: bfloat16 [32, 512, 128], P(None, 'blk'), may hold values from -6 to 6
- routes: int32 [4, 4], replicated, may hold values from 0 to 7
Outputs:
- query_grad: bfloat16 [32, 4096, 128], P(None, ('blk', 'ulysses'))
- key_grad: float32 [32, 512, 128], P(None, ('blk', 'ulysses'))
- value_grad: float32 [32, 512, 128], P(None, ('blk', 'ulysses'))
All inputs are finite; a program needn't handle non-finite values.
Results may differ from a plain program's by a relative error of at most 0.0056.
Values may be sent and summed in bfloat16 or wider, within the bound.
No kernel may reach another device: no remote copies, remote signals or barrier semaphores. Data moves between devices by JAX's collectives and lax.ppermute only.
A program may use at most 64 MiB of HBM per device.

v0:
```python
import math
import jax
import jax.numpy as jnp
from jax import lax
from jax.sharding import PartitionSpec as P

KB = 16


def body(query_rows, out_grad, key_rows, value_rows, routes):
    head_count, token_count, head_dim = query_rows.shape
    group_keys = key_rows.shape[1]
    cycle_size = lax.axis_size("blk")
    group_size = lax.axis_size("ulysses")
    sub_count = max(1, group_size // head_count)
    item_count = head_count * sub_count // group_size
    sub_length = token_count // sub_count
    row_count = group_size * sub_length
    block_count = group_keys // KB
    key_stride = token_count * group_size // group_keys
    score_scale = 1.0 / math.sqrt(head_dim)
    my_group = lax.axis_index("blk")
    my_rank = lax.axis_index("ulysses")
    packed_query = query_rows.reshape(head_count * sub_count, sub_length, head_dim)
    packed_grad = out_grad.reshape(head_count * sub_count, sub_length, head_dim)
    local_query, local_grad = (
        lax.all_to_all(packed_query, "ulysses", split_axis=0, concat_axis=1, tiled=True),
        lax.all_to_all(packed_grad, "ulysses", split_axis=0, concat_axis=1, tiled=True),
    )
    first_head = my_rank * item_count // sub_count
    own_keys = lax.dynamic_slice_in_dim(key_rows, first_head, item_count, 0)
    own_values = lax.dynamic_slice_in_dim(value_rows, first_head, item_count, 0)
    requested = lax.dynamic_index_in_dim(routes, my_group, 1, keepdims=False)
    block_ids = jnp.arange(block_count, dtype=jnp.int32)
    block_keys = own_keys.reshape(item_count, block_count, KB, head_dim)
    block_values = own_values.reshape(item_count, block_count, KB, head_dim)
    far_keys, far_values = (
        lax.all_to_all(
            jnp.take(block_keys, requested, axis=1), "blk", split_axis=1, concat_axis=1, tiled=True
        ),
        lax.all_to_all(
            jnp.take(block_values, requested, axis=1),
            "blk",
            split_axis=1,
            concat_axis=1,
            tiled=True,
        ),
    )
    near_keys = jnp.concatenate(
        [own_keys, far_keys.reshape(item_count, cycle_size * KB, head_dim)], axis=1
    )
    near_values = jnp.concatenate(
        [own_values, far_values.reshape(item_count, cycle_size * KB, head_dim)], axis=1
    )
    near_count = near_keys.shape[1]
    item_sub = (my_rank * item_count + jnp.arange(item_count, dtype=jnp.int32)) % sub_count
    far_visible = jnp.repeat(jnp.arange(cycle_size, dtype=jnp.int32) < my_group, KB)
    own_offsets = jnp.arange(group_keys, dtype=jnp.int32) * key_stride
    block_rows = 1024

    def attend(row_block, carried):
        query_out, key_acc, value_acc = carried
        row_start = row_block * block_rows
        queries = lax.dynamic_slice_in_dim(local_query, row_start, block_rows, 1)
        grad_rows = lax.dynamic_slice_in_dim(local_grad, row_start, block_rows, 1)
        row_ids = row_start + jnp.arange(block_rows, dtype=jnp.int32)
        positions = (
            row_ids[None, :] // sub_length * token_count
            + item_sub[:, None] * sub_length
            + row_ids[None, :] % sub_length
        )
        own_visible = own_offsets[None, None, :] <= positions[:, :, None]
        visible = jnp.concatenate(
            [
                own_visible,
                jnp.broadcast_to(far_visible, (item_count, block_rows, far_visible.shape[0])),
            ],
            axis=2,
        )
        scores = (
            jnp.einsum("ird,ikd->irk", queries, near_keys, preferred_element_type=jnp.float32)
            * score_scale
        )
        row_max = jnp.max(jnp.where(visible, scores, -jnp.inf), axis=-1, keepdims=True)
        expsum = jnp.where(visible, jnp.exp(scores - row_max), 0.0)
        weights = expsum / jnp.sum(expsum, axis=-1, keepdims=True)
        weights_half = weights.astype(jnp.bfloat16)
        attended = jnp.einsum(
            "irk,ikd->ird", weights_half, near_values, preferred_element_type=jnp.float32
        )
        delta_rows = jnp.sum(grad_rows.astype(jnp.float32) * attended, axis=-1, keepdims=True)
        dweights = jnp.einsum(
            "ird,ikd->irk", grad_rows, near_values, preferred_element_type=jnp.float32
        )
        dscore = (weights * (dweights - delta_rows)).astype(jnp.bfloat16)
        query_part = (
            jnp.einsum("irk,ikd->ird", dscore, near_keys, preferred_element_type=jnp.float32)
            * score_scale
        ).astype(jnp.bfloat16)
        key_acc = (
            key_acc
            + jnp.einsum("irk,ird->ikd", dscore, queries, preferred_element_type=jnp.float32)
            * score_scale
        )
        value_acc = value_acc + jnp.einsum(
            "irk,ird->ikd", weights_half, grad_rows, preferred_element_type=jnp.float32
        )
        query_out = lax.dynamic_update_slice_in_dim(query_out, query_part, row_start, 1)
        return (query_out, key_acc, value_acc)

    start_state = (
        jnp.zeros((item_count, row_count, head_dim), jnp.bfloat16),
        jnp.zeros((item_count, near_count, head_dim), jnp.float32),
        jnp.zeros((item_count, near_count, head_dim), jnp.float32),
    )
    query_out, key_acc, value_acc = lax.fori_loop(0, row_count // block_rows, attend, start_state)
    own_key_grad = key_acc[:, :group_keys]
    own_value_grad = value_acc[:, :group_keys]
    far_key_grad = key_acc[:, group_keys:].reshape(item_count, cycle_size, KB, head_dim)
    far_value_grad = value_acc[:, group_keys:].reshape(item_count, cycle_size, KB, head_dim)
    back_keys, back_values = (
        lax.all_to_all(far_key_grad, "blk", split_axis=1, concat_axis=1, tiled=True),
        lax.all_to_all(far_value_grad, "blk", split_axis=1, concat_axis=1, tiled=True),
    )
    placer = (requested[:, None] == block_ids[None, :]).astype(jnp.float32)
    added_keys = jnp.einsum(
        "gb,igkd->ibkd", placer, back_keys, precision=lax.Precision.HIGHEST
    ).reshape(item_count, group_keys, head_dim)
    added_values = jnp.einsum(
        "gb,igkd->ibkd", placer, back_values, precision=lax.Precision.HIGHEST
    ).reshape(item_count, group_keys, head_dim)
    key_share = (own_key_grad + added_keys).astype(jnp.bfloat16)
    value_share = (own_value_grad + added_values).astype(jnp.bfloat16)
    query_back, key_back, value_back = (
        lax.all_to_all(query_out, "ulysses", split_axis=1, concat_axis=0, tiled=True),
        lax.all_to_all(key_share, "ulysses", split_axis=1, concat_axis=0, tiled=True),
        lax.all_to_all(value_share, "ulysses", split_axis=1, concat_axis=0, tiled=True),
    )
    query_grad = query_back.reshape(head_count, token_count, head_dim)
    key_grad = jnp.sum(
        key_back.astype(jnp.float32).reshape(head_count, sub_count, -1, head_dim), axis=1
    )
    value_grad = jnp.sum(
        value_back.astype(jnp.float32).reshape(head_count, sub_count, -1, head_dim), axis=1
    )
    return (query_grad, key_grad, value_grad)


def solution(mesh):
    return jax.shard_map(
        body,
        mesh=mesh,
        in_specs=(
            P(None, ("blk", "ulysses"), None),
            P(None, ("blk", "ulysses"), None),
            P(None, "blk", None),
            P(None, "blk", None),
            P(),
        ),
        out_specs=(
            P(None, ("blk", "ulysses"), None),
            P(None, ("blk", "ulysses"), None),
            P(None, ("blk", "ulysses"), None),
        ),
        check_vma=False,
    )
```

profile of v0, /device:TPU:0, one launch (start us, length us, event | category | flops | bytes accessed | tf_op | source)
XLA Modules:
  0.0 155.4 jit_solution(3819428733041253633)
XLA Ops:
  1.5 1.0 constant_dynamic-slice_fusion
  3.8 8.2 %all_to_all.92 = bf16[4,4,16,128]{3,2,0,1:T(8,128)(2,1)S(1)} all-to-all(bf16[4,4,16,128]{3,2,0,1:T(8,128)(2,1)S(1)} %get-tuple-element.29), channel_id=1, replica_groups=mesh['blk'=4,'ulysses'=8] {'blk'}, dimensions={1} | all-to-all | bytes 131072 | tf_op jit(solution)/shard_map/all_to_all | solution.py:38
  11.9 6.5 %all_to_all.93 = bf16[4,4,16,128]{3,2,0,1:T(8,128)(2,1)S(1)} all-to-all(bf16[4,4,16,128]{3,2,0,1:T(8,128)(2,1)S(1)} %get-tuple-element.28), channel_id=1, replica_groups=mesh['blk'=4,'ulysses'=8] {'blk'}, dimensions={1} | all-to-all | bytes 131072 | tf_op jit(solution)/shard_map/all_to_all | solution.py:41
  18.4 31.4 %all_to_all.94 = bf16[32,128,128]{2,1,0:T(8,128)(2,1)S(1)} all-to-all(bf16[32,128,128]{2,1,0:T(8,128)(2,1)} %param.7), channel_id=1, replica_groups=mesh['blk'=4,'ulysses'=8] {'ulysses'}, dimensions={0} | all-to-all | bytes 2097152 | tf_op jit(solution)/shard_map/all_to_all | solution.py:27
  49.8 3.6 %all-to-all-start.3 = ((bf16[32,128,128]{2,1,0:T(8,128)(2,1)}), bf16[32,128,128]{2,1,0:T(8,128)(2,1)S(1)}, u32[]{:S(2)}, u32[]{:S(2)}) async-start(bf16[32,128,128]{2,1,0:T(8,128)(2,1)} %param.8), calls=%async_computation.3 | async-start | bytes 2097152 | tf_op jit(solution)/shard_map/all_to_all | solution.py:28
  53.6 1.0 broadcast_compare_fusion
  55.4 23.6 %all-to-all-done.3 = bf16[32,128,128]{2,1,0:T(8,128)(2,1)S(1)} async-done(((bf16[32,128,128]{2,1,0:T(8,128)(2,1)}), bf16[32,128,128]{2,1,0:T(8,128)(2,1)S(1)}, u32[]{:S(2)}, u32[]{:S(2)}) %all-to-all-start.3) | async-done | bytes 1048608 | tf_op jit(solution)/shard_map/all_to_all | solution.py:28
  79.0 1.0 copy.33
  80.0 4.5 %fusion.40 = (f32[4,1024]{1,0:T(4,128)S(1)}, f32[4,1024,192]{1,2,0:T(8,128)}) fusion(pred[4,1024,128]{1,2,0:T(32,128)(4,1)} %broadcast_compare_fusion, pred[192]{0:T(512)(128)(4,1)S(1)} %pad.5.clone, bf16[4,1024,128]{2,1,0:T(8,128)(2,1)S(1)} %bitcast.73, bf16[4,64,128]{2,1,0:T(8,128)(2,1)S(1)} %bitcast.90, bf16[4,128,128]{2,1,0:T(8,128)(2,1)S(1)} %get-tuple-element.33), kind=kOutput, calls=%fused_computation.69 | convolution fusion | flops 409731264 | bytes 4931776 | tf_op jit(solution)/shard_map/while/body/eval_jaxpr/sub | solution.py:85
  84.6 2.4 %fusion.8 = bf16[4,1024,192]{1,2,0:T(8,128)(2,1)S(1)} fusion(f32[4,1024,192]{1,2,0:T(8,128)} %get-tuple-element.31, f32[4,1024]{1,0:T(4,128)S(1)} %get-tuple-element.30), kind=kLoop, calls=%fused_computation.17 | loop fusion | flops 1572864 | bytes 4734976 | tf_op jit(solution)/shard_map/while/body/eval_jaxpr/convert_element_type | solution.py:87
  88.2 3.3 %all-to-all-start.7 = ((f32[4,4,16,128]{3,2,0,1:T(8,128)}), f32[4,4,16,128]{3,2,0,1:T(8,128)S(1)}, u32[]{:S(2)}, u32[]{:S(2)}) async-start(f32[4,4,16,128]{3,2,0,1:T(8,128)} %copy.42), calls=%async_computation.7 | async-start | bytes 262144 | tf_op jit(solution)/shard_map/all_to_all | solution.py:123
  91.6 2.5 %multiply_reduce_fusion = f32[4,1024]{1,0:T(4,128)S(1)} fusion(bf16[4,1024,128]{2,1,0:T(8,128)(2,1)} %bitcast.75, bf16[4,1024,192]{1,2,0:T(8,128)(2,1)S(1)} %fusion.8, bf16[4,64,128]{2,1,0:T(8,128)(2,1)S(1)} %bitcast.92, bf16[4,128,128]{2,1,0:T(8,128)(2,1)S(1)} %copy-done.6), kind=kOutput, calls=%fused_computation.12 | convolution fusion | flops 203288576 | bytes 2834432 | tf_op jit(solution)/shard_map/while/body/eval_jaxpr/irk,ikd->ird/dot_general | solution.py:88
  94.1 2.5 %fusion.1 = bf16[4,1024,192]{1,2,0:T(8,128)(2,1)S(1)} fusion(bf16[4,1024,128]{2,1,0:T(8,128)(2,1)S(1)} %bitcast.77, f32[4,1024]{1,0:T(4,128)S(1)} %multiply_reduce_fusion, f32[4,1024,192]{1,2,0:T(8,128)} %get-tuple-element.31, f32[4,1024]{1,0:T(4,128)S(1)} %get-tuple-element.30, bf16[4,64,128]{2,1,0:T(8,128)(2,1)S(1)} %bitcast.93, ...), kind=kOutput, calls=%fused_computation.4 | convolution fusion | flops 204865536 | bytes 5996544 | tf_op jit(solution)/shard_map/while/body/eval_jaxpr/ird,ikd->irk/dot_general | solution.py:92
  97.9 3.3 %all-to-all-start.5 = ((f32[4,4,16,128]{3,2,0,1:T(8,128)}), f32[4,4,16,128]{3,2,0,1:T(8,128)S(1)}, u32[]{:S(2)}, u32[]{:S(2)}) async-start(f32[4,4,16,128]{3,2,0,1:T(8,128)} %copy.37), calls=%async_computation.5 | async-start | bytes 262144 | tf_op jit(solution)/shard_map/all_to_all | solution.py:122
  102.5 3.3 %all-to-all-done.5 = f32[4,4,16,128]{3,2,0,1:T(8,128)S(1)} async-done(((f32[4,4,16,128]{3,2,0,1:T(8,128)}), f32[4,4,16,128]{3,2,0,1:T(8,128)S(1)}, u32[]{:S(2)}, u32[]{:S(2)}) %all-to-all-start.5) | async-done | bytes 131104 | tf_op jit(solution)/shard_map/all_to_all | solution.py:122
  105.8 3.4 %all-to-all-start.8 = ((bf16[4,128,128]{2,0,1:T(4,128)(2,1)}), bf16[4,128,128]{2,0,1:T(4,128)(2,1)S(1)}, u32[]{:S(2)}, u32[]{:S(2)}) async-start(bf16[4,128,128]{2,0,1:T(4,128)(2,1)} %copy.45), calls=%async_computation.8 | async-start | bytes 262144 | tf_op jit(solution)/shard_map/all_to_all | solution.py:137
  110.5 6.1 %all-to-all-done.8 = bf16[4,128,128]{2,0,1:T(4,128)(2,1)S(1)} async-done(((bf16[4,128,128]{2,0,1:T(4,128)(2,1)}), bf16[4,128,128]{2,0,1:T(4,128)(2,1)S(1)}, u32[]{:S(2)}, u32[]{:S(2)}) %all-to-all-start.8) | async-done | bytes 131104 | tf_op jit(solution)/shard_map/all_to_all | solution.py:137
  116.6 3.4 %all-to-all-start.6 = ((bf16[4,128,128]{2,0,1:T(4,128)(2,1)}), bf16[4,128,128]{2,0,1:T(4,128)(2,1)S(1)}, u32[]{:S(2)}, u32[]{:S(2)}) async-start(bf16[4,128,128]{2,0,1:T(4,128)(2,1)} %copy.40), calls=%async_computation.6 | async-start | bytes 262144 | tf_op jit(solution)/shard_map/all_to_all | solution.py:136
  120.0 1.0 multiply_convert_fusion
  120.9 1.8 %copy.35 = bf16[4,1024,128]{2,0,1:T(4,128)(2,1)} copy(bf16[4,1024,128]{2,1,0:T(8,128)(2,1)S(1)} %multiply_convert_fusion) | data formatting | bytes 2097152 | tf_op jit(solution)/shard_map/while/body/eval_jaxpr/convert_element_type | solution.py:99
  122.7 4.5 %all-to-all-done.6 = bf16[4,128,128]{2,0,1:T(4,128)(2,1)S(1)} async-done(((bf16[4,128,128]{2,0,1:T(4,128)(2,1)}), bf16[4,128,128]{2,0,1:T(4,128)(2,1)S(1)}, u32[]{:S(2)}, u32[]{:S(2)}) %all-to-all-start.6) | async-done | bytes 131104 | tf_op jit(solution)/shard_map/all_to_all | solution.py:136
  127.2 3.6 %all-to-all-start.4 = ((bf16[4,1024,128]{2,0,1:T(4,128)(2,1)}), bf16[4,1024,128]{2,0,1:T(4,128)(2,1)S(1)}, u32[]{:S(2)}, u32[]{:S(2)}) async-start(bf16[4,1024,128]{2,0,1:T(4,128)(2,1)} %copy.35), calls=%async_computation.4 | async-start | bytes 2097152 | tf_op jit(solution)/shard_map/all_to_all | solution.py:135
  132.3 21.9 %all-to-all-done.4 = bf16[4,1024,128]{2,0,1:T(4,128)(2,1)S(1)} async-done(((bf16[4,1024,128]{2,0,1:T(4,128)(2,1)}), bf16[4,1024,128]{2,0,1:T(4,128)(2,1)S(1)}, u32[]{:S(2)}, u32[]{:S(2)}) %all-to-all-start.4) | async-done | bytes 1048608 | tf_op jit(solution)/shard_map/all_to_all | solution.py:135
  154.2 1.2 copy.36
  (55 shorter events, 9.5 us)
Async XLA Ops:
  0.6 0.7 copy-start
  2.5 52.8 %copy-start.5 = (bf16[4,128,128]{2,1,0:T(8,128)(2,1)}, bf16[4,128,128]{2,1,0:T(8,128)(2,1)S(1)}, u32[]{:S(2)}) copy-start(bf16[4,128,128]{2,1,0:T(8,128)(2,1)S(1)} %get-tuple-element.32) | copy-start | bytes 393220
  2.5 77.5 %copy-start.3 = (bf16[4,128,128]{2,1,0:T(8,128)(2,1)}, bf16[4,128,128]{2,1,0:T(8,128)(2,1)S(1)}, u32[]{:S(2)}) copy-start(bf16[4,128,128]{2,1,0:T(8,128)(2,1)S(1)} %get-tuple-element.33) | copy-start | bytes 393220
  49.8 29.2 %all-to-all-start.3 = ((bf16[32,128,128]{2,1,0:T(8,128)(2,1)}), bf16[32,128,128]{2,1,0:T(8,128)(2,1)S(1)}, u32[]{:S(2)}, u32[]{:S(2)}) async-start(bf16[32,128,128]{2,1,0:T(8,128)(2,1)} %param.8), calls=%async_computation.3 | async-start | bytes 2097152 | tf_op jit(solution)/shard_map/all_to_all | solution.py:28
  54.6 29.9 %copy-start.7 = (bf16[4,4,16,128]{3,2,1,0:T(8,128)(2,1)}, bf16[4,4,16,128]{3,2,1,0:T(8,128)(2,1)S(1)}, u32[]{:S(2)}) copy-start(bf16[4,4,16,128]{3,2,1,0:T(8,128)(2,1)S(1)} %copy.30) | copy-start | bytes 196612
  84.5 2.5 %copy-start.1 = (bf16[8,4,128,128]{3,2,0,1:T(8,128)(2,1)S(1)}, bf16[8,4,128,128]{3,2,0,1:T(8,128)(2,1)}, u32[]{:S(2)}) copy-start(bf16[8,4,128,128]{3,2,0,1:T(8,128)(2,1)} %copy.33) | copy-start | bytes 3145732
  84.5 7.1 %copy-start.6 = (bf16[4,128,128]{2,1,0:T(8,128)(2,1)S(1)}, bf16[4,128,128]{2,1,0:T(8,128)(2,1)}, u32[]{:S(2)}) copy-start(bf16[4,128,128]{2,1,0:T(8,128)(2,1)} %copy-done.5) | copy-start | bytes 393220
  84.5 7.1 %copy-start.9 = (bf16[4,4,16,128]{3,2,1,0:T(8,128)(2,1)S(1)}, bf16[4,4,16,128]{3,2,1,0:T(8,128)(2,1)}, u32[]{:S(2)}) copy-start(bf16[4,4,16,128]{3,2,1,0:T(8,128)(2,1)} %copy.32) | copy-start | bytes 196612
  88.2 9.6 %all-to-all-start.7 = ((f32[4,4,16,128]{3,2,0,1:T(8,128)}), f32[4,4,16,128]{3,2,0,1:T(8,128)S(1)}, u32[]{:S(2)}, u32[]{:S(2)}) async-start(f32[4,4,16,128]{3,2,0,1:T(8,128)} %copy.42), calls=%async_computation.7 | async-start | bytes 262144 | tf_op jit(solution)/shard_map/all_to_all | solution.py:123
  91.6 2.5 %copy-start.2 = (bf16[8,4,128,128]{3,2,0,1:T(8,128)(2,1)S(1)}, bf16[8,4,128,128]{3,2,0,1:T(8,128)(2,1)}, u32[]{:S(2)}) copy-start(bf16[8,4,128,128]{3,2,0,1:T(8,128)(2,1)} %copy.33) | copy-start | bytes 3145732
  97.2 22.8 %copy-start.4 = (bf16[4,128,128]{2,1,0:T(8,128)(2,1)S(1)}, bf16[4,128,128]{2,1,0:T(8,128)(2,1)}, u32[]{:S(2)}) copy-start(bf16[4,128,128]{2,1,0:T(8,128)(2,1)} %copy-done.3) | copy-start | bytes 393220
  97.2 22.8 %copy-start.8 = (bf16[4,4,16,128]{3,2,1,0:T(8,128)(2,1)S(1)}, bf16[4,4,16,128]{3,2,1,0:T(8,128)(2,1)}, u32[]{:S(2)}) copy-start(bf16[4,4,16,128]{3,2,1,0:T(8,128)(2,1)} %copy-done.7) | copy-start | bytes 196612
  97.9 7.9 %all-to-all-start.5 = ((f32[4,4,16,128]{3,2,0,1:T(8,128)}), f32[4,4,16,128]{3,2,0,1:T(8,128)S(1)}, u32[]{:S(2)}, u32[]{:S(2)}) async-start(f32[4,4,16,128]{3,2,0,1:T(8,128)} %copy.37), calls=%async_computation.5 | async-start | bytes 262144 | tf_op jit(solution)/shard_map/all_to_all | solution.py:122
  105.8 10.8 %all-to-all-start.8 = ((bf16[4,128,128]{2,0,1:T(4,128)(2,1)}), bf16[4,128,128]{2,0,1:T(4,128)(2,1)S(1)}, u32[]{:S(2)}, u32[]{:S(2)}) async-start(bf16[4,128,128]{2,0,1:T(4,128)(2,1)} %copy.45), calls=%async_computation.8 | async-start | bytes 262144 | tf_op jit(solution)/shard_map/all_to_all | solution.py:137
  116.6 10.7 %all-to-all-start.6 = ((bf16[4,128,128]{2,0,1:T(4,128)(2,1)}), bf16[4,128,128]{2,0,1:T(4,128)(2,1)S(1)}, u32[]{:S(2)}, u32[]{:S(2)}) async-start(bf16[4,128,128]{2,0,1:T(4,128)(2,1)} %copy.40), calls=%async_computation.6 | async-start | bytes 262144 | tf_op jit(solution)/shard_map/all_to_all | solution.py:136
  127.2 26.9 %all-to-all-start.4 = ((bf16[4,1024,128]{2,0,1:T(4,128)(2,1)}), bf16[4,1024,128]{2,0,1:T(4,128)(2,1)S(1)}, u32[]{:S(2)}, u32[]{:S(2)}) async-start(bf16[4,1024,128]{2,0,1:T(4,128)(2,1)} %copy.35), calls=%async_computation.4 | async-start | bytes 2097152 | tf_op jit(solution)/shard_map/all_to_all | solution.py:135
where the time goes:
time: 156 us; the launch traced here: 155 us
  waiting for transfers between devices  59.4 us (38%)
  blocking collectives  46 us (29%)
  starting transfers between devices  20.6 us (13%)
  local copies, waits for them, and re-layouts  12.4 us (8%)
  matrix products  12.4 us (8%)
  other arithmetic  3.66 us (2%)
    all_to_all x1, blocking collectives, body(): lax.all_to_all(packed_query, 'ulysses', split_axis=0, concat_axis=1, tile...  31.4 us
    all_to_all x1, waiting for transfers between devices, body(): lax.all_to_all(packed_grad, 'ulysses', split_axis=0, concat_axis=1, tiled...  23.6 us
    all_to_all x1, waiting for transfers between devices, body(): lax.all_to_all(query_out, 'ulysses', split_axis=1, concat_axis=0, tiled=T...  21.9 us
    all_to_all x1, blocking collectives, body(): lax.all_to_all(jnp.take(block_keys, requested, axis=1), 'blk', split_axis...  8.16 us
    all_to_all x1, blocking collectives, body(): lax.all_to_all(jnp.take(block_values, requested, axis=1), 'blk', split_ax...  6.47 us
    all_to_all x1, waiting for transfers between devices, body(): lax.all_to_all(value_share, 'ulysses', split_axis=1, concat_axis=0, tiled...  6.08 us
    all_to_all x1, waiting for transfers between devices, body(): lax.all_to_all(key_share, 'ulysses', split_axis=1, concat_axis=0, tiled=T...  4.52 us
    sub x1, matrix products, attend(): expsum = jnp.where(visible, jnp.exp(scores - row_max), 0.0)  4.49 us
  transfers between devices with their start and end apart: 6, of which 5 were waited for; matrix products, arithmetic and copies ran while one was open for 10% of the time, Pallas kernels for 0%

commit v1 on v0

--- a/solution.py
+++ b/solution.py
@@ -5,6 +5,40 @@
 from jax.sharding import PartitionSpec as P
 
 KB = 16
+
+
+def supply_all_the_terms(message, out_dim, tile_in):
+    local_part = message.shape
+    part_now = message.reshape(
+        *local_part[:out_dim], tile_in, local_part[out_dim] // tile_in, *local_part[out_dim + 1 :]
+    )
+    top = jnp.moveaxis(part_now, out_dim, 0)
+    return top
+
+
+def return_all_the_side(sheet, axis_no):
+    sheet = jnp.moveaxis(sheet, 0, axis_no)
+    step_out = sheet.shape
+    carry_out = sheet.reshape(
+        *step_out[:axis_no], step_out[axis_no] * step_out[axis_no + 1], *step_out[axis_no + 2 :]
+    )
+    return carry_out
+
+
+def sheets_meet(original, shard_axis, page, z_in):
+    val = lax.psum(1, shard_axis)
+    finding, met_up = (val, lax.axis_index(shard_axis))
+    local_next = supply_all_the_terms(original, page, finding)
+    tmp = local_next
+    for c in tuple(range(1, finding)):
+        y2, moved = ((met_up + c) % finding, (met_up - c) % finding)
+        arr_out = lax.dynamic_index_in_dim(local_next, y2, 0)
+        out_arr = lax.ppermute(
+            arr_out, shard_axis, [(t, (t + c) % finding) for t in range(finding)]
+        )
+        tmp = lax.dynamic_update_slice_in_dim(tmp, out_arr, moved, axis=0)
+    v1 = return_all_the_side(tmp, z_in)
+    return v1
 
 
 def body(query_rows, out_grad, key_rows, value_rows, routes):
@@ -25,7 +59,7 @@
     packed_grad = out_grad.reshape(head_count * sub_count, sub_length, head_dim)
     local_query, local_grad = (
         lax.all_to_all(packed_query, "ulysses", split_axis=0, concat_axis=1, tiled=True),
-        lax.all_to_all(packed_grad, "ulysses", split_axis=0, concat_axis=1, tiled=True),
+        sheets_meet(packed_grad, "ulysses", page=0, z_in=1),
     )
     first_head = my_rank * item_count // sub_count
     own_keys = lax.dynamic_slice_in_dim(key_rows, first_head, item_count, 0)

time: 156 us -> 204 us (1.31)
  local copies, waits for them, and re-layouts: 12.4 us -> 59.5 us
  blocking collectives: 46 us -> 14.6 us
  starting transfers between devices: 20.6 us -> 42.1 us
  waiting for transfers between devices: 59.4 us -> 75.1 us
  matrix products: 12.4 us -> 7.34 us
    dynamic_update_slice x0 -> x7, local copies, waits for them, and re-layouts: none -> 41.8 us  [sheets_meet(): tmp = lax.dynamic_update_slice_in_dim(tmp, out_arr, moved, axis=0)]
    ppermute x0 -> x7, waiting for transfers between devices: none -> 35.9 us  [sheets_meet(): lax.ppermute(arr_out, shard_axis, [(t, (t + c) % finding) for t in range(...]
    all_to_all x1 -> x0, blocking collectives: 31.4 us -> none  [body(): lax.all_to_all(packed_query, 'ulysses', split_axis=0, concat_axis=1, tile...]
    all_to_all x1, waiting for transfers between devices: 23.6 us -> 0.01 us  [body(): lax.all_to_all(packed_query, 'ulysses', split_axis=0, concat_axis=1, tile...]
    ppermute x0 -> x7, starting transfers between devices: none -> 19.3 us  [sheets_meet(): lax.ppermute(arr_out, shard_axis, [(t, (t + c) % finding) for t in range(...]
    all_to_all x1, waiting for transfers between devices: 0.01 us -> 3.3 us  [body(): lax.all_to_all(far_value_grad, 'blk', split_axis=1, concat_axis=1, tiled=...]
    dynamic_slice x0 -> x1, local copies, waits for them, and re-layouts: none -> 2.78 us  [sheets_meet(): arr_out = lax.dynamic_index_in_dim(local_next, y2, 0)]
    all_to_all x1, starting transfers between devices: 3.59 us -> 5.83 us  [body(): lax.all_to_all(packed_query, 'ulysses', split_axis=0, concat_axis=1, tile...]
  transfers between devices with their start and end apart: 6 -> 13, of which waited for: 5 -> 7; matrix products, arithmetic and copies ran while one was open for 10% -> 27% of each run, Pallas kernels for 0% -> 0%
where the time goes in v1:
time: 204 us; the launch traced here: 203 us
  waiting for transfers between devices  75.1 us (37%)
  local copies, waits for them, and re-layouts  59.5 us (29%)
  starting transfers between devices  42.1 us (21%)
  blocking collectives  14.6 us (7%)
  matrix products  7.34 us (4%)
  other arithmetic  2.89 us (1%)
    dynamic_update_slice x7, local copies, waits for them, and re-layouts, sheets_meet(): tmp = lax.dynamic_update_slice_in_dim(tmp, out_arr, moved, axis=0)  41.8 us
    ppermute x7, waiting for transfers between devices, sheets_meet(): lax.ppermute(arr_out, shard_axis, [(t, (t + c) % finding) for t in range(...  35.9 us
    all_to_all x1, waiting for transfers between devices, body(): lax.all_to_all(query_out, 'ulysses', split_axis=1, concat_axis=0, tiled=T...  22.1 us
    ppermute x7, starting transfers between devices, sheets_meet(): lax.ppermute(arr_out, shard_axis, [(t, (t + c) % finding) for t in range(...  19.3 us
    all_to_all x1, blocking collectives, body(): lax.all_to_all(jnp.take(block_values, requested, axis=1), 'blk', split_ax...  8.16 us
    all_to_all x1, blocking collectives, body(): lax.all_to_all(jnp.take(block_keys, requested, axis=1), 'blk', split_axis...  6.47 us
    all_to_all x1, waiting for transfers between devices, body(): lax.all_to_all(key_share, 'ulysses', split_axis=1, concat_axis=0, tiled=T...  6.02 us
    all_to_all x1, starting transfers between devices, body(): lax.all_to_all(packed_query, 'ulysses', split_axis=0, concat_axis=1, tile...  5.83 us
  transfers between devices with their start and end apart: 13, of which 7 were waited for; matrix products, arithmetic and copies ran while one was open for 27% of the time, Pallas kernels for 0%

profile of v1, /device:TPU:0, one launch (start us, length us, event | category | flops | bytes accessed | tf_op | source)
XLA Modules:
  0.0 202.7 jit_solution(9597339206591309734)
XLA Ops:
  3.8 8.2 %all_to_all.74 = bf16[4,4,16,128]{3,2,0,1:T(8,128)(2,1)S(1)} all-to-all(bf16[4,4,16,128]{3,2,0,1:T(8,128)(2,1)S(1)} %get-tuple-element.35), channel_id=1, replica_groups=mesh['blk'=4,'ulysses'=8] {'blk'}, dimensions={1} | all-to-all | bytes 131072 | tf_op jit(solution)/shard_map/all_to_all | solution.py:75
  11.9 6.5 %all_to_all.75 = bf16[4,4,16,128]{3,2,0,1:T(8,128)(2,1)S(1)} all-to-all(bf16[4,4,16,128]{3,2,0,1:T(8,128)(2,1)S(1)} %get-tuple-element.48), channel_id=1, replica_groups=mesh['blk'=4,'ulysses'=8] {'blk'}, dimensions={1} | all-to-all | bytes 131072 | tf_op jit(solution)/shard_map/all_to_all | solution.py:72
  18.4 5.8 %all-to-all-start.1 = ((bf16[32,128,128]{2,1,0:T(8,128)(2,1)}), bf16[32,128,128]{2,1,0:T(8,128)(2,1)}, u32[]{:S(2)}, u32[]{:S(2)}) async-start(bf16[32,128,128]{2,1,0:T(8,128)(2,1)} %param.7), calls=%async_computation.1 | async-start | bytes 2097152 | tf_op jit(solution)/shard_map/all_to_all | solution.py:61
  27.8 4.7 %collective-permute-start.6 = (bf16[1,4,128,128]{2,0,3,1:T(2,128)(2,1)}, bf16[1,4,128,128]{2,0,3,1:T(2,128)(2,1)S(1)}, u32[]{:S(2)}, u32[]{:S(2)}) collective-permute-start(bf16[1,4,128,128]{2,0,3,1:T(2,128)(2,1)} %get-tuple-element.28), channel_id=1, source_target_pairs={{0,7},{1,0},{2,1},{3,2},{4,3},{5,4},{6,5},{7,6},{8,15},{9,8},{10,9... | collective-permute-start | bytes 393224 | tf_op jit(solution)/shard_map/ppermute | solution.py:36
  36.7 30.9 %collective-permute-done.1 = bf16[1,4,128,128]{2,0,3,1:T(2,128)(2,1)S(1)} collective-permute-done((bf16[1,4,128,128]{2,0,3,1:T(2,128)(2,1)S(1)}, bf16[1,4,128,128]{2,0,3,1:T(2,128)(2,1)S(1)}, u32[]{:S(2)}, u32[]{:S(2)}) %collective-permute-start.1) | collective-permute-done | bytes 131104 | tf_op jit(solution)/shard_map/ppermute | solution.py:36
  67.7 10.5 %collective-permute-start.3 = (bf16[1,4,128,128]{2,0,3,1:T(2,128)(2,1)}, bf16[1,4,128,128]{2,0,3,1:T(2,128)(2,1)S(1)}, u32[]{:S(2)}, u32[]{:S(2)}) collective-permute-start(bf16[1,4,128,128]{2,0,3,1:T(2,128)(2,1)} %get-tuple-element.31), channel_id=1, source_target_pairs={{0,4},{1,5},{2,6},{3,7},{4,0},{5,1},{6,2},{7,3},{8,12},{9,13},{10,... | collective-permute-start | bytes 393224 | tf_op jit(solution)/shard_map/ppermute | solution.py:36
  79.0 5.9 %dynamic_update_slice.23 = bf16[8,4,128,128]{2,0,3,1:T(8,128)(2,1)S(1)} dynamic-update-slice(bf16[8,4,128,128]{2,0,3,1:T(8,128)(2,1)S(1)} %copy.49, bf16[1,4,128,128]{2,0,3,1:T(2,128)(2,1)S(1)} %collective-permute-done, s32[]{:T(128)S(6)} %select_n.170, s32[]{:T(128)} %constant.187.clone.1, s32[]{:T(128)} %constant.187.clone.1, s32[]{:T(128)} %constant.187.clone.1) | dynamic-update-slice | bytes 262148 | tf_op jit(solution)/shard_map/dynamic_update_slice | solution.py:39
  84.9 5.9 %dynamic_update_slice.24 = bf16[8,4,128,128]{2,0,3,1:T(8,128)(2,1)S(1)} dynamic-update-slice(bf16[8,4,128,128]{2,0,3,1:T(8,128)(2,1)S(1)} %dynamic_update_slice.23, bf16[1,4,128,128]{2,0,3,1:T(2,128)(2,1)S(1)} %collective-permute-done.1, s32[]{:T(128)S(6)} %select_n.174, s32[]{:T(128)} %constant.187.clone.1, s32[]{:T(128)} %constant.187.clone.1, s32[]{:T(128)} %constant.187.clone.1) | dynamic-update-slice | bytes 262148 | tf_op jit(solution)/shard_map/dynamic_update_slice | solution.py:39
  90.8 4.9 %collective-permute-done.2 = bf16[1,4,128,128]{2,0,3,1:T(2,128)(2,1)} collective-permute-done((bf16[1,4,128,128]{2,0,3,1:T(2,128)(2,1)}, bf16[1,4,128,128]{2,0,3,1:T(2,128)(2,1)}, u32[]{:S(2)}, u32[]{:S(2)}) %collective-permute-start.2) | collective-permute-done | bytes 131104 | tf_op jit(solution)/shard_map/ppermute | solution.py:36
  95.7 6.6 %dynamic_update_slice.25 = bf16[8,4,128,128]{2,0,3,1:T(8,128)(2,1)S(1)} dynamic-update-slice(bf16[8,4,128,128]{2,0,3,1:T(8,128)(2,1)S(1)} %dynamic_update_slice.24, bf16[1,4,128,128]{2,0,3,1:T(2,128)(2,1)} %collective-permute-done.2, s32[]{:T(128)S(6)} %select_n.178, s32[]{:T(128)} %constant.187.clone.1, s32[]{:T(128)} %constant.187.clone.1, s32[]{:T(128)} %constant.187.clone.1) | dynamic-update-slice | bytes 262148 | tf_op jit(solution)/shard_map/dynamic_update_slice | solution.py:39
  102.3 5.9 %dynamic_update_slice.26 = bf16[8,4,128,128]{2,0,3,1:T(8,128)(2,1)S(1)} dynamic-update-slice(bf16[8,4,128,128]{2,0,3,1:T(8,128)(2,1)S(1)} %dynamic_update_slice.25, bf16[1,4,128,128]{2,0,3,1:T(2,128)(2,1)S(1)} %collective-permute-done.3, s32[]{:T(128)S(6)} %select_n.182, s32[]{:T(128)} %constant.187.clone.1, s32[]{:T(128)} %constant.187.clone.1, s32[]{:T(128)} %constant.187.clone.1) | dynamic-update-slice | bytes 262148 | tf_op jit(solution)/shard_map/dynamic_update_slice | solution.py:39
  108.2 5.9 %dynamic_update_slice.27 = bf16[8,4,128,128]{2,0,3,1:T(8,128)(2,1)S(1)} dynamic-update-slice(bf16[8,4,128,128]{2,0,3,1:T(8,128)(2,1)S(1)} %dynamic_update_slice.26, bf16[1,4,128,128]{2,0,3,1:T(2,128)(2,1)S(1)} %collective-permute-done.4, s32[]{:T(128)S(6)} %select_n.186, s32[]{:T(128)} %constant.187.clone.1, s32[]{:T(128)} %constant.187.clone.1, s32[]{:T(128)} %constant.187.clone.1) | dynamic-update-slice | bytes 262148 | tf_op jit(solution)/shard_map/dynamic_update_slice | solution.py:39
  114.1 5.9 %dynamic_update_slice.28 = bf16[8,4,128,128]{2,0,3,1:T(8,128)(2,1)S(1)} dynamic-update-slice(bf16[8,4,128,128]{2,0,3,1:T(8,128)(2,1)S(1)} %dynamic_update_slice.27, bf16[1,4,128,128]{2,0,3,1:T(2,128)(2,1)S(1)} %collective-permute-done.5, s32[]{:T(128)S(6)} %select_n.190, s32[]{:T(128)} %constant.187.clone.1, s32[]{:T(128)} %constant.187.clone.1, s32[]{:T(128)} %constant.187.clone.1) | dynamic-update-slice | bytes 262148 | tf_op jit(solution)/shard_map/dynamic_update_slice | solution.py:39
  120.0 5.9 %dynamic_update_slice.29 = bf16[8,4,128,128]{2,0,3,1:T(8,128)(2,1)S(1)} dynamic-update-slice(bf16[8,4,128,128]{2,0,3,1:T(8,128)(2,1)S(1)} %dynamic_update_slice.28, bf16[1,4,128,128]{2,0,3,1:T(2,128)(2,1)S(1)} %collective-permute-done.6, s32[]{:T(128)S(6)} %select_n.194, s32[]{:T(128)} %constant.187.clone.1, s32[]{:T(128)} %constant.187.clone.1, s32[]{:T(128)} %constant.187.clone.1) | dynamic-update-slice | bytes 262148 | tf_op jit(solution)/shard_map/dynamic_update_slice | solution.py:39
  127.7 3.3 %fusion.41 = (f32[4,1024]{1,0:T(4,128)S(1)}, f32[4,1024,192]{1,2,0:T(8,128)}) fusion(pred[4,1024,128]{1,2,0:T(32,128)(4,1)S(1)} %broadcast_compare_fusion, pred[192]{0:T(512)(128)(4,1)S(1)} %pad.5.clone, bf16[4,1024,128]{2,1,0:T(8,128)(2,1)S(1)} %bitcast.72, bf16[4,64,128]{2,1,0:T(8,128)(2,1)S(1)} %bitcast.85, bf16[4,128,128]{2,1,0:T(8,128)(2,1)S(1)} %get-tuple-element.52), kind=kOutput, calls=%fused_computation.77 | convolution fusion | flops 409731264 | bytes 4931776 | tf_op jit(solution)/shard_map/while/body/eval_jaxpr/sub | solution.py:119
  137.2 3.3 %all-to-all-start.4 = ((f32[4,4,16,128]{3,2,0,1:T(8,128)}), f32[4,4,16,128]{3,2,0,1:T(8,128)S(1)}, u32[]{:S(2)}, u32[]{:S(2)}) async-start(f32[4,4,16,128]{3,2,0,1:T(8,128)} %copy.60), calls=%async_computation.4 | async-start | bytes 262144 | tf_op jit(solution)/shard_map/all_to_all | solution.py:156
  145.1 3.3 %all-to-all-start.6 = ((f32[4,4,16,128]{3,2,0,1:T(8,128)}), f32[4,4,16,128]{3,2,0,1:T(8,128)S(1)}, u32[]{:S(2)}, u32[]{:S(2)}) async-start(f32[4,4,16,128]{3,2,0,1:T(8,128)} %copy.66), calls=%async_computation.6 | async-start | bytes 262144 | tf_op jit(solution)/shard_map/all_to_all | solution.py:157
  149.7 3.3 %all-to-all-done.6 = f32[4,4,16,128]{3,2,0,1:T(8,128)S(1)} async-done(((f32[4,4,16,128]{3,2,0,1:T(8,128)}), f32[4,4,16,128]{3,2,0,1:T(8,128)S(1)}, u32[]{:S(2)}, u32[]{:S(2)}) %all-to-all-start.6) | async-done | bytes 131104 | tf_op jit(solution)/shard_map/all_to_all | solution.py:157
  153.0 3.4 %all-to-all-start.5 = ((bf16[4,128,128]{2,0,1:T(4,128)(2,1)}), bf16[4,128,128]{2,0,1:T(4,128)(2,1)S(1)}, u32[]{:S(2)}, u32[]{:S(2)}) async-start(bf16[4,128,128]{2,0,1:T(4,128)(2,1)} %copy.63), calls=%async_computation.5 | async-start | bytes 262144 | tf_op jit(solution)/shard_map/all_to_all | solution.py:170
  157.6 6.0 %all-to-all-done.5 = bf16[4,128,128]{2,0,1:T(4,128)(2,1)S(1)} async-done(((bf16[4,128,128]{2,0,1:T(4,128)(2,1)}), bf16[4,128,128]{2,0,1:T(4,128)(2,1)S(1)}, u32[]{:S(2)}, u32[]{:S(2)}) %all-to-all-start.5) | async-done | bytes 131104 | tf_op jit(solution)/shard_map/all_to_all | solution.py:170
  163.6 3.4 %all-to-all-start.7 = ((bf16[4,128,128]{2,0,1:T(4,128)(2,1)}), bf16[4,128,128]{2,0,1:T(4,128)(2,1)S(1)}, u32[]{:S(2)}, u32[]{:S(2)}) async-start(bf16[4,128,128]{2,0,1:T(4,128)(2,1)} %copy.69), calls=%async_computation.7 | async-start | bytes 262144 | tf_op jit(solution)/shard_map/all_to_all | solution.py:171
  169.8 4.5 %all-to-all-done.7 = bf16[4,128,128]{2,0,1:T(4,128)(2,1)S(1)} async-done(((bf16[4,128,128]{2,0,1:T(4,128)(2,1)}), bf16[4,128,128]{2,0,1:T(4,128)(2,1)S(1)}, u32[]{:S(2)}, u32[]{:S(2)}) %all-to-all-start.7) | async-done | bytes 131104 | tf_op jit(solution)/shard_map/all_to_all | solution.py:171
  174.3 3.6 %all-to-all-start.3 = ((bf16[4,1024,128]{2,0,1:T(4,128)(2,1)}), bf16[4,1024,128]{2,0,1:T(4,128)(2,1)S(1)}, u32[]{:S(2)}, u32[]{:S(2)}) async-start(bf16[4,1024,128]{2,0,1:T(4,128)(2,1)} %copy.58), calls=%async_computation.3 | async-start | bytes 2097152 | tf_op jit(solution)/shard_map/all_to_all | solution.py:169
  179.3 22.1 %all-to-all-done.3 = bf16[4,1024,128]{2,0,1:T(4,128)(2,1)S(1)} async-done(((bf16[4,1024,128]{2,0,1:T(4,128)(2,1)}), bf16[4,1024,128]{2,0,1:T(4,128)(2,1)S(1)}, u32[]{:S(2)}, u32[]{:S(2)}) %all-to-all-start.3) | async-done | bytes 1048608 | tf_op jit(solution)/shard_map/all_to_all | solution.py:169
  (81 shorter events, 32.0 us)
Async XLA Ops:
  0.6 23.6 %copy-start.6 = (bf16[32,128,128]{2,1,0:T(8,128)(2,1)S(1)}, bf16[32,128,128]{2,1,0:T(8,128)(2,1)}, u32[]{:S(2)}) copy-start(bf16[32,128,128]{2,1,0:T(8,128)(2,1)} %param.8) | copy-start | bytes 3145732
  2.5 125.2 %copy-start.7 = (bf16[4,128,128]{2,1,0:T(8,128)(2,1)}, bf16[4,128,128]{2,1,0:T(8,128)(2,1)S(1)}, u32[]{:S(2)}) copy-start(bf16[4,128,128]{2,1,0:T(8,128)(2,1)S(1)} %get-tuple-element.52) | copy-start | bytes 393220
  18.4 108.0 %all-to-all-start.1 = ((bf16[32,128,128]{2,1,0:T(8,128)(2,1)}), bf16[32,128,128]{2,1,0:T(8,128)(2,1)}, u32[]{:S(2)}, u32[]{:S(2)}) async-start(bf16[32,128,128]{2,1,0:T(8,128)(2,1)} %param.7), calls=%async_computation.1 | async-start | bytes 2097152 | tf_op jit(solution)/shard_map/all_to_all | solution.py:61
  27.8 92.2 %collective-permute-start.6 = (bf16[1,4,128,128]{2,0,3,1:T(2,128)(2,1)}, bf16[1,4,128,128]{2,0,3,1:T(2,128)(2,1)S(1)}, u32[]{:S(2)}, u32[]{:S(2)}) collective-permute-start(bf16[1,4,128,128]{2,0,3,1:T(2,128)(2,1)} %get-tuple-element.28), channel_id=1, source_target_pairs={{0,7},{1,0},{2,1},{3,2},{4,3},{5,4},{6,5},{7,6},{8,15},{9,8},{10,9... | collective-permute-start | bytes 393224 | tf_op jit(solution)/shard_map/ppermute | solution.py:36
  32.5 81.6 %collective-permute-start.5 = (bf16[1,4,128,128]{2,0,3,1:T(2,128)(2,1)}, bf16[1,4,128,128]{2,0,3,1:T(2,128)(2,1)S(1)}, u32[]{:S(2)}, u32[]{:S(2)}) collective-permute-start(bf16[1,4,128,128]{2,0,3,1:T(2,128)(2,1)} %get-tuple-element.29), channel_id=1, source_target_pairs={{0,6},{1,7},{2,0},{3,1},{4,2},{5,3},{6,4},{7,5},{8,14},{9,15},{10,... | collective-permute-start | bytes 393224 | tf_op jit(solution)/shard_map/ppermute | solution.py:36
  33.1 75.1 %collective-permute-start.4 = (bf16[1,4,128,128]{2,0,3,1:T(2,128)(2,1)}, bf16[1,4,128,128]{2,0,3,1:T(2,128)(2,1)S(1)}, u32[]{:S(2)}, u32[]{:S(2)}) collective-permute-start(bf16[1,4,128,128]{2,0,3,1:T(2,128)(2,1)} %get-tuple-element.30), channel_id=1, source_target_pairs={{0,5},{1,6},{2,7},{3,0},{4,1},{5,2},{6,3},{7,4},{8,13},{9,14},{10,... | collective-permute-start | bytes 393224 | tf_op jit(solution)/shard_map/ppermute | solution.py:36
  33.1 34.6 %collective-permute-start.1 = (bf16[1,4,128,128]{2,0,3,1:T(2,128)(2,1)S(1)}, bf16[1,4,128,128]{2,0,3,1:T(2,128)(2,1)S(1)}, u32[]{:S(2)}, u32[]{:S(2)}) collective-permute-start(bf16[1,4,128,128]{2,0,3,1:T(2,128)(2,1)S(1)} %get-tuple-element.33), channel_id=1, source_target_pairs={{0,2},{1,3},{2,4},{3,5},{4,6},{5,7},{6,0},{7,1},{8,10},{9,11},{10,... | collective-permute-start | bytes 393224 | tf_op jit(solution)/shard_map/ppermute | solution.py:36
  34.5 43.7 %collective-permute-start = (bf16[1,4,128,128]{2,0,3,1:T(2,128)(2,1)S(1)}, bf16[1,4,128,128]{2,0,3,1:T(2,128)(2,1)S(1)}, u32[]{:S(2)}, u32[]{:S(2)}) collective-permute-start(bf16[1,4,128,128]{2,0,3,1:T(2,128)(2,1)S(1)} %get-tuple-element.34), channel_id=1, source_target_pairs={{0,1},{1,2},{2,3},{3,4},{4,5},{5,6},{6,7},{7,0},{8,9},{9,10},{10,1... | collective-permute-start | bytes 393224 | tf_op jit(solution)/shard_map/ppermute | solution.py:36
  67.7 34.6 %collective-permute-start.3 = (bf16[1,4,128,128]{2,0,3,1:T(2,128)(2,1)}, bf16[1,4,128,128]{2,0,3,1:T(2,128)(2,1)S(1)}, u32[]{:S(2)}, u32[]{:S(2)}) collective-permute-start(bf16[1,4,128,128]{2,0,3,1:T(2,128)(2,1)} %get-tuple-element.31), channel_id=1, source_target_pairs={{0,4},{1,5},{2,6},{3,7},{4,0},{5,1},{6,2},{7,3},{8,12},{9,13},{10,... | collective-permute-start | bytes 393224 | tf_op jit(solution)/shard_map/ppermute | solution.py:36
  78.2 17.5 %collective-permute-start.2 = (bf16[1,4,128,128]{2,0,3,1:T(2,128)(2,1)}, bf16[1,4,128,128]{2,0,3,1:T(2,128)(2,1)}, u32[]{:S(2)}, u32[]{:S(2)}) collective-permute-start(bf16[1,4,128,128]{2,0,3,1:T(2,128)(2,1)} %get-tuple-element.32), channel_id=1, source_target_pairs={{0,3},{1,4},{2,5},{3,6},{4,7},{5,0},{6,1},{7,2},{8,11},{9,12},{10,... | collective-permute-start | bytes 393224 | tf_op jit(solution)/shard_map/ppermute | solution.py:36
  79.0 48.7 %copy-start.9 = (bf16[4,4,16,128]{3,2,1,0:T(8,128)(2,1)}, bf16[4,4,16,128]{3,2,1,0:T(8,128)(2,1)S(1)}, u32[]{:S(2)}) copy-start(bf16[4,4,16,128]{3,2,1,0:T(8,128)(2,1)S(1)} %copy.46) | copy-start | bytes 196612
  127.7 3.3 %copy-start.1 = (bf16[8,4,128,128]{3,2,0,1:T(8,128)(2,1)}, bf16[8,4,128,128]{3,2,0,1:T(8,128)(2,1)S(1)}, u32[]{:S(2)}) copy-start(bf16[8,4,128,128]{3,2,0,1:T(8,128)(2,1)S(1)} %copy.47) | copy-start | bytes 3145732
  131.0 2.5 %copy-start.11 = (bf16[4,4,16,128]{3,2,1,0:T(8,128)(2,1)S(1)}, bf16[4,4,16,128]{3,2,1,0:T(8,128)(2,1)}, u32[]{:S(2)}) copy-start(bf16[4,4,16,128]{3,2,1,0:T(8,128)(2,1)} %copy.56) | copy-start | bytes 196612
  131.0 3.1 %copy-start.3 = (f32[4,1024,192]{1,2,0:T(8,128)S(1)}, f32[4,1024,192]{1,2,0:T(8,128)}, u32[]{:S(2)}) copy-start(f32[4,1024,192]{1,2,0:T(8,128)} %get-tuple-element.50) | copy-start | bytes 9437188
  134.1 1.2 copy-start.2
  135.3 1.2 copy-start.4
  137.2 7.9 %all-to-all-start.4 = ((f32[4,4,16,128]{3,2,0,1:T(8,128)}), f32[4,4,16,128]{3,2,0,1:T(8,128)S(1)}, u32[]{:S(2)}, u32[]{:S(2)}) async-start(f32[4,4,16,128]{3,2,0,1:T(8,128)} %copy.60), calls=%async_computation.4 | async-start | bytes 262144 | tf_op jit(solution)/shard_map/all_to_all | solution.py:156
  141.1 25.9 %copy-start.5 = (bf16[4,1024,192]{1,2,0:T(8,128)(2,1)S(1)}, bf16[4,1024,192]{1,2,0:T(8,128)(2,1)}, u32[]{:S(2)}) copy-start(bf16[4,1024,192]{1,2,0:T(8,128)(2,1)} %copy-done.4) | copy-start | bytes 4718596
  141.1 25.9 %copy-start.8 = (bf16[4,128,128]{2,1,0:T(8,128)(2,1)S(1)}, bf16[4,128,128]{2,1,0:T(8,128)(2,1)}, u32[]{:S(2)}) copy-start(bf16[4,128,128]{2,1,0:T(8,128)(2,1)} %copy-done.7) | copy-start | bytes 393220
  141.1 25.9 %copy-start.10 = (bf16[4,4,16,128]{3,2,1,0:T(8,128)(2,1)S(1)}, bf16[4,4,16,128]{3,2,1,0:T(8,128)(2,1)}, u32[]{:S(2)}) copy-start(bf16[4,4,16,128]{3,2,1,0:T(8,128)(2,1)} %copy-done.9) | copy-start | bytes 196612
  145.1 7.9 %all-to-all-start.6 = ((f32[4,4,16,128]{3,2,0,1:T(8,128)}), f32[4,4,16,128]{3,2,0,1:T(8,128)S(1)}, u32[]{:S(2)}, u32[]{:S(2)}) async-start(f32[4,4,16,128]{3,2,0,1:T(8,128)} %copy.66), calls=%async_computation.6 | async-start | bytes 262144 | tf_op jit(solution)/shard_map/all_to_all | solution.py:157
  153.0 10.7 %all-to-all-start.5 = ((bf16[4,128,128]{2,0,1:T(4,128)(2,1)}), bf16[4,128,128]{2,0,1:T(4,128)(2,1)S(1)}, u32[]{:S(2)}, u32[]{:S(2)}) async-start(bf16[4,128,128]{2,0,1:T(4,128)(2,1)} %copy.63), calls=%async_computation.5 | async-start | bytes 262144 | tf_op jit(solution)/shard_map/all_to_all | solution.py:170
  163.6 10.7 %all-to-all-start.7 = ((bf16[4,128,128]{2,0,1:T(4,128)(2,1)}), bf16[4,128,128]{2,0,1:T(4,128)(2,1)S(1)}, u32[]{:S(2)}, u32[]{:S(2)}) async-start(bf16[4,128,128]{2,0,1:T(4,128)(2,1)} %copy.69), calls=%async_computation.7 | async-start | bytes 262144 | tf_op jit(solution)/shard_map/all_to_all | solution.py:171
  174.3 27.2 %all-to-all-start.3 = ((bf16[4,1024,128]{2,0,1:T(4,128)(2,1)}), bf16[4,1024,128]{2,0,1:T(4,128)(2,1)S(1)}, u32[]{:S(2)}, u32[]{:S(2)}) async-start(bf16[4,1024,128]{2,0,1:T(4,128)(2,1)} %copy.58), calls=%async_computation.3 | async-start | bytes 2097152 | tf_op jit(solution)/shard_map/all_to_all | solution.py:169
  (1 other events, 0.7 us)
